TPU v7x, 512 devices: a whole 4x4x16 slice. The times are simulated.
512 devices in a mesh: feeder: 32 (over x, y, core), scen: 16 (over z).
Axes of the slice: x: 4, y: 4, z: 16, core: 2. Of those that a mesh axis runs over, the one named last changes fastest.
Arguments:
- anchor: bfloat16 [256, 24, 16384], P('scen', None, 'feeder'), may hold values from -6 to 6
- cost_lin: bfloat16 [256, 24, 16384], P('scen', None, 'feeder'), may hold values from -6 to 6
- dual: float32 [256, 24, 16384], P('scen', None, 'feeder'), may hold values from -4 to 4
- target: float32 [256, 24], P('scen'), may hold values from -4 to 4
- leaf_weight: float32 [256], P('scen'), may hold values from 1 to 10
- q_mat: bfloat16 [16384, 512], P('feeder'), may hold values from -0.25 to 0.25
- diag_gain: float32 [16384], P('feeder'), may hold values from 0.5 to 2
- block_mask: int32 [32, 4, 4], P('feeder'), may hold values from 0 to 1, as said below
- ancestor: int32 [24, 256], P(None, 'scen'), may hold values from 0 to 255, as said below
Outputs:
- setpoints: float32 [256, 24, 16384], P('scen', None, 'feeder')
- average: float32 [256, 24, 16384], P('scen', None, 'feeder')
- new_dual: float32 [256, 24, 16384], P('scen', None, 'feeder')
Inputs may be any that keep to these rules, and one draw needn't show every extreme that they name: `block_mask`: every diagonal block is present; the share of present off-diagonal blocks differs from feeder to feeder. ancestor[t, s] is the first leaf of the section-t tree node that holds leaf s: the leaves of a node are consecutive, ancestor[0, s] = 0, and every section-t node lies inside one section-(t-1) node. Nodes may span several groups at any section.
All inputs are finite; a program needn't handle non-finite values.
Results may differ from a plain program's by a relative error of at most 0.0003.
Values sent between devices are 32-bit elements; how exact they have to be, the bound alone decides.
No kernel may reach another device: no remote copies, remote signals or barrier semaphores. Data moves between devices by JAX's collectives and lax.ppermute only.
A program may use at most 64 MiB of HBM per device.

v0:
```python
import jax
import jax.numpy as jnp
from jax import lax
from jax.sharding import PartitionSpec as P

PROX_ITERS = 8
penalty = 1.0
step_size = 0.08
coupling = 4.0
power_limit = 2.0


def link_terms(earlier, later):
    return (
        later[0] + later[2][:, None] * earlier[0],
        later[1] + later[2] * earlier[1],
        earlier[2] * later[2],
    )


def local(anchor, cost_lin, dual, target, leaf_weight, q_mat, diag_gain, block_mask, ancestor):
    leaves, sections, nodes = anchor.shape
    rows = leaves * sections
    count = block_mask.shape[1]
    width = nodes // count
    total_nodes = lax.axis_size("feeder") * nodes
    start_pt = anchor.astype(jnp.float32)
    fixed_part = cost_lin.astype(jnp.float32) + dual - penalty * start_pt
    diag_term = 2.0 * diag_gain + penalty
    expand = jnp.repeat(jnp.repeat(block_mask[0], width, axis=0), width, axis=1).astype(
        jnp.bfloat16
    )
    q_eff = q_mat * expand
    state = start_pt
    for sweep in range(PROX_ITERS):
        flat = state.reshape(rows, nodes).astype(jnp.bfloat16)
        image = jnp.dot(flat, q_eff, preferred_element_type=jnp.float32)
        head = lax.psum(jnp.sum(state, axis=2), "feeder") / total_nodes
        grad = image.reshape(leaves, sections, nodes) + diag_term * state + fixed_part
        grad = grad + coupling * (head - target)[:, :, None]
        state = jnp.clip(state - step_size * grad, -power_limit, power_limit)
    highest = lax.Precision.HIGHEST
    weighted = leaf_weight[:, None, None] * state
    first_leaf = lax.axis_index("scen") * leaves
    local_id = jnp.maximum(ancestor - first_leaf, 0)
    slot_ids = jnp.arange(leaves, dtype=jnp.int32)
    member = (local_id[:, None, :] == slot_ids[None, :, None]).astype(jnp.float32)
    seg_sums = jnp.einsum("tgl,ltn->tgn", member, weighted, precision=highest)
    seg_weights = jnp.einsum("tgl,l->tg", member, leaf_weight, precision=highest)
    last_pick = (slot_ids[None, :] == local_id[:, leaves - 1][:, None]).astype(jnp.float32)
    first_pick = (slot_ids[None, :] == 0).astype(jnp.float32)
    tail_sum = jnp.einsum("tg,tgn->tn", last_pick, seg_sums, precision=highest)
    tail_weight = jnp.sum(last_pick * seg_weights, axis=1)
    continued = (ancestor[:, 0] < first_leaf).astype(jnp.float32)
    spanning = (ancestor[:, leaves - 1] < first_leaf).astype(jnp.float32)
    head_sum = seg_sums[:, 0, :] * continued[:, None]
    head_weight = seg_weights[:, 0] * continued
    gathered = (
        lax.all_gather(tail_sum[None], "scen", axis=0, tiled=True),
        lax.all_gather(tail_weight[None], "scen", axis=0, tiled=True),
        lax.all_gather(head_sum[None], "scen", axis=0, tiled=True),
        lax.all_gather(head_weight[None], "scen", axis=0, tiled=True),
        lax.all_gather(spanning[None], "scen", axis=0, tiled=True),
    )
    position = lax.axis_index("scen")
    group_ids = jnp.arange(gathered[0].shape[0], dtype=jnp.int32)
    blank = (jnp.zeros_like(tail_sum), jnp.zeros_like(tail_weight), jnp.ones_like(spanning))

    def forward_step(carry, item):
        group, part_sum, part_weight, part_flag = item
        joined = link_terms(carry, (part_sum, part_weight, part_flag))
        keep = group < position
        return (
            jax.tree.map(lambda new_val, old_val: jnp.where(keep, new_val, old_val), joined, carry),
            None,
        )

    def backward_step(carry, item):
        group, part_sum, part_weight, part_flag = item
        joined = link_terms(carry, (part_sum, part_weight, part_flag))
        keep = group > position
        return (
            jax.tree.map(lambda new_val, old_val: jnp.where(keep, new_val, old_val), joined, carry),
            None,
        )

    before, unused = lax.scan(
        forward_step, blank, (group_ids, gathered[0], gathered[1], gathered[4])
    )
    after, unused = lax.scan(
        backward_step, blank, (group_ids, gathered[2], gathered[3], gathered[4]), reverse=True
    )
    open_front = first_pick * continued[:, None]
    seg_total = (
        seg_sums
        + open_front[:, :, None] * before[0][:, None, :]
        + last_pick[:, :, None] * after[0][:, None, :]
    )
    weight_total = seg_weights + open_front * before[1][:, None] + last_pick * after[1][:, None]
    leaf_sums = jnp.einsum("tgl,tgn->ltn", member, seg_total, precision=highest)
    leaf_weights = jnp.einsum("tgl,tg->lt", member, weight_total, precision=highest)
    average = leaf_sums / leaf_weights[:, :, None]
    new_dual = dual + penalty * (state - average)
    return (state, average, new_dual)


def solution(mesh):
    return jax.shard_map(
        local,
        mesh=mesh,
        in_specs=(
            P("scen", None, "feeder"),
            P("scen", None, "feeder"),
            P("scen", None, "feeder"),
            P("scen", None),
            P("scen"),
            P("feeder", None),
            P("feeder"),
            P("feeder", None, None),
            P(None, "scen"),
        ),
        out_specs=(P("scen", None, "feeder"), P("scen", None, "feeder"), P("scen", None, "feeder")),
        check_vma=False,
    )
```

profile of v0, /device:TPU:32, one launch (start us, length us, event | category | flops | bytes accessed | tf_op | source)
XLA Modules:
  0.0 681.2 jit_solution(15530600553333728089)
XLA Ops:
  0.6 0.7 convert_bitcast_fusion
  2.1 0.9 copy-done
  3.9 68.3 %psum.56 = f32[16,24]{1,0:T(8,128)S(1)} all-reduce(f32[16,24]{1,0:T(8,128)S(1)} %convert_reduce_fusion), channel_id=1, replica_groups=mesh['feeder'=32,'scen'=16] {'feeder'}, use_global_device_ids=true, to_apply=%region_1.0 | all-reduce | flops 384 | bytes 3072 | tf_op jit(solution)/shard_map/psum | solution.py:38
  72.2 1.4 fusion.74
  73.6 63.7 %psum.57 = f32[16,24]{1,0:T(8,128)S(1)} all-reduce(f32[16,24]{1,0:T(8,128)S(1)} %get-tuple-element.314), channel_id=1, replica_groups=mesh['feeder'=32,'scen'=16] {'feeder'}, use_global_device_ids=true, to_apply=%region_3.4 | all-reduce | flops 384 | bytes 3072 | tf_op jit(solution)/shard_map/psum | solution.py:38
  137.4 0.9 fusion.93
  138.2 63.7 %psum.58 = f32[16,24]{1,0:T(8,128)S(1)} all-reduce(f32[16,24]{1,0:T(8,128)S(1)} %get-tuple-element.320), channel_id=1, replica_groups=mesh['feeder'=32,'scen'=16] {'feeder'}, use_global_device_ids=true, to_apply=%region_5.6 | all-reduce | flops 384 | bytes 3072 | tf_op jit(solution)/shard_map/psum | solution.py:38
  202.5 63.7 %psum.59 = f32[16,24]{1,0:T(8,128)S(1)} all-reduce(f32[16,24]{1,0:T(8,128)S(1)} %get-tuple-element.322), channel_id=1, replica_groups=mesh['feeder'=32,'scen'=16] {'feeder'}, use_global_device_ids=true, to_apply=%region_7.8 | all-reduce | flops 384 | bytes 3072 | tf_op jit(solution)/shard_map/psum | solution.py:38
  266.8 63.7 %psum.60 = f32[16,24]{1,0:T(8,128)S(1)} all-reduce(f32[16,24]{1,0:T(8,128)S(1)} %get-tuple-element.324), channel_id=1, replica_groups=mesh['feeder'=32,'scen'=16] {'feeder'}, use_global_device_ids=true, to_apply=%region_9.10 | all-reduce | flops 384 | bytes 3072 | tf_op jit(solution)/shard_map/psum | solution.py:38
  331.1 63.7 %psum.61 = f32[16,24]{1,0:T(8,128)S(1)} all-reduce(f32[16,24]{1,0:T(8,128)S(1)} %get-tuple-element.326), channel_id=1, replica_groups=mesh['feeder'=32,'scen'=16] {'feeder'}, use_global_device_ids=true, to_apply=%region_11.12 | all-reduce | flops 384 | bytes 3072 | tf_op jit(solution)/shard_map/psum | solution.py:38
  394.8 1.4 fusion.97
  396.1 63.7 %psum.62 = f32[16,24]{1,0:T(8,128)S(1)} all-reduce(f32[16,24]{1,0:T(8,128)S(1)} %get-tuple-element.328), channel_id=1, replica_groups=mesh['feeder'=32,'scen'=16] {'feeder'}, use_global_device_ids=true, to_apply=%region_13.14 | all-reduce | flops 384 | bytes 3072 | tf_op jit(solution)/shard_map/psum | solution.py:38
  459.8 2.0 fusion.98
  461.8 63.7 %psum.63 = f32[16,24]{1,0:T(8,128)S(1)} all-reduce(f32[16,24]{1,0:T(8,128)S(1)} %get-tuple-element.330), channel_id=1, replica_groups=mesh['feeder'=32,'scen'=16] {'feeder'}, use_global_device_ids=true, to_apply=%region_15.16 | all-reduce | flops 384 | bytes 3072 | tf_op jit(solution)/shard_map/psum | solution.py:38
  526.2 1.4 broadcast_multiply_fusion
  527.5 0.7 copy-done.6
  528.3 1.0 fusion.48
  529.9 37.7 %all-gather = f32[384,512]{1,0:T(8,128)S(1)} all-gather(f32[24,512]{1,0:T(8,128)S(1)} %bitcast.122), channel_id=2, replica_groups=mesh['feeder'=32,'scen'=16] {'scen'}, dimensions={0}, use_global_device_ids=true | all-gather | bytes 835584 | tf_op jit(solution)/shard_map/all_gather | solution.py:59
  568.0 1.3 dynamic-slice
  570.3 30.1 %all-reduce.3 = (f32[384]{0:T(512)S(1)}, f32[384]{0:T(512)S(1)}, f32[384]{0:T(512)S(1)}) all-reduce(f32[384]{0:T(512)S(1)} %fusion.86, f32[384]{0:T(512)S(1)} %fusion.84, f32[384]{0:T(512)S(1)} %dynamic-update-slice.1), channel_id=3, replica_groups=mesh['feeder'=32,'scen'=16] {'scen'}, use_global_device_ids=true, to_apply=%add | all-reduce | flops 1152 | bytes 9216
  600.6 23.5 %while.30 = (s32[]{:T(128)}, f32[24,512]{1,0:T(8,128)S(1)}, f32[24]{0:T(128)S(1)}, s32[16]{0:T(128)S(1)}, s32[]{:T(128)}, /*index=5*/f32[16,24,512]{2,1,0:T(8,12...) while((s32[]{:T(128)}, f32[24,512]{1,0:T(8,128)S(1)}, ...), condition=%wide.region_18.19_spmd.clone, body=%wide.region_17.18_spmd.clone.sunk | while | flops 49252 | bytes 148175 | solution.py:87
  600.6 0.7 dynamic_slice.91
  603.5 0.7 dynamic_slice.91
  605.0 0.7 dynamic_slice.91
  609.4 0.7 dynamic_slice.91
  610.9 0.7 dynamic_slice.91
  612.3 0.7 dynamic_slice.91
  624.2 30.1 %all_gather.18 = f32[16,24,512]{2,1,0:T(8,128)S(1)} all-gather(f32[1,24,512]{2,1,0:T(8,128)S(1)} %copy.24), channel_id=1, replica_groups=mesh['feeder'=32,'scen'=16] {'scen'}, dimensions={0}, use_global_device_ids=true | all-gather | bytes 835584 | tf_op jit(solution)/shard_map/all_gather | solution.py:61
  654.4 23.5 %while.31 = (s32[]{:T(128)}, f32[24,512]{1,0:T(8,128)S(1)}, f32[24]{0:T(128)S(1)}, s32[16]{0:T(128)S(1)}, s32[]{:T(128)}, /*index=5*/f32[16,24,512]{2,1,0:T(8,12...) while((s32[]{:T(128)}, f32[24,512]{1,0:T(8,128)S(1)}, ...), condition=%wide.region_20.21_spmd.clone, body=%wide.region_19.20_spmd.clone.sunk | while | flops 49253 | bytes 148195 | solution.py:90
  654.4 0.7 dynamic_slice.94
  678.2 0.7 fusion.50
  679.5 1.7 subtract_add_fusion
  (157 shorter events, 26.3 us)
Async XLA Ops:
  0.6 1.4 copy-start.4
  2.0 1.0 copy-start
  3.0 0.7 copy-start.7
  3.0 69.2 %copy-start.2 = (f32[16,24,512]{2,1,0:T(8,128)S(1)}, f32[16,24,512]{2,1,0:T(8,128)}, u32[]{:S(2)}) copy-start(f32[16,24,512]{2,1,0:T(8,128)} %param.15) | copy-start | bytes 2359300
  3.8 68.4 %copy-start.5 = (f32[16,24]{1,0:T(8,128)S(1)}, f32[16,24]{1,0:T(8,128)}, u32[]{:S(2)}) copy-start(f32[16,24]{1,0:T(8,128)} %param.16) | copy-start | bytes 4612
  525.5 0.7 copy-start.8
  527.5 0.7 copy-start.6
  678.2 1.1 copy-start.1
  678.2 1.4 copy-start.3
where the time goes:
time: 682 us; the launch traced here: 681 us
  blocking collectives  612 us (90%)
  local copies, waits for them, and re-layouts  27 us (4%)
  loops' own time  22.6 us (3%)
  matrix products  10.1 us (1%)
  other arithmetic  7.87 us (1%)
    psum x8, blocking collectives, local(): head = lax.psum(jnp.sum(state, axis=2), 'feeder') / total_nodes  514 us
    all_gather x1, blocking collectives, local(): lax.all_gather(tail_sum[None], 'scen', axis=0, tiled=True)  37.7 us
    all_gather x1, blocking collectives, local(): lax.all_gather(head_sum[None], 'scen', axis=0, tiled=True)  30.1 us
    unnamed x1, blocking collectives  30.1 us
    dynamic_slice x32, local copies, waits for them, and re-layouts, local(): lax.scan(forward_step, blank, (group_ids, gathered[0], gathered[1], gathe...  21.2 us

commit v1 on v0

--- a/solution.py
+++ b/solution.py
@@ -8,6 +8,11 @@
 step_size = 0.08
 coupling = 4.0
 power_limit = 2.0
+
+
+def add_all(x, axis):
+    parts = lax.all_gather(x, axis)
+    return jnp.sum(parts, axis=0)
 
 
 def link_terms(earlier, later):
@@ -35,7 +40,7 @@
     for sweep in range(PROX_ITERS):
         flat = state.reshape(rows, nodes).astype(jnp.bfloat16)
         image = jnp.dot(flat, q_eff, preferred_element_type=jnp.float32)
-        head = lax.psum(jnp.sum(state, axis=2), "feeder") / total_nodes
+        head = add_all(jnp.sum(state, axis=2), "feeder") / total_nodes
         grad = image.reshape(leaves, sections, nodes) + diag_term * state + fixed_part
         grad = grad + coupling * (head - target)[:, :, None]
         state = jnp.clip(state - step_size * grad, -power_limit, power_limit)

time: 682 us -> 359 us (0.53)
  the two profiles are of different devices: /device:TPU:32 before, /device:TPU:4 now
where the time goes in v1:
time: 359 us; the launch traced here: 358 us
  blocking collectives  288 us (80%)
  local copies, waits for them, and re-layouts  27.7 us (8%)
  loops' own time  22.6 us (6%)
  matrix products  10.2 us (3%)
  other arithmetic  8.21 us (2%)
    all_gather x8, blocking collectives, add_all(): parts = lax.all_gather(x, axis)  191 us
    all_gather x1, blocking collectives, local(): lax.all_gather(tail_sum[None], 'scen', axis=0, tiled=True)  37.2 us
    all_gather x1, blocking collectives, local(): lax.all_gather(head_sum[None], 'scen', axis=0, tiled=True)  32.1 us
    unnamed x1, blocking collectives  27.5 us
    dynamic_slice x32, local copies, waits for them, and re-layouts, local(): lax.scan(forward_step, blank, (group_ids, gathered[0], gathered[1], gathe...  21.2 us
    another operation x1, loops' own time, local(): lax.scan(backward_step, blank, (group_ids, gathered[2], gathered[3], gath...  11.3 us
    another operation x1, loops' own time, local(): lax.scan(forward_step, blank, (group_ids, gathered[0], gathered[1], gathe...  11.3 us
    dot_general x8, matrix products, local(): image = jnp.dot(flat, q_eff, preferred_element_type=jnp.float32)  7.77 us

profile of v1, /device:TPU:4, one launch (start us, length us, event | category | flops | bytes accessed | tf_op | source)
XLA Modules:
  0.0 358.4 jit_solution(13315539829135253379)
XLA Ops:
  0.6 0.7 convert_bitcast_fusion
  2.1 0.9 copy-done
  3.8 25.7 %all-gather = f32[512,24]{1,0:T(8,128)S(1)} all-gather(f32[16,24]{1,0:T(8,128)S(1)} %convert_reduce_fusion), channel_id=2, replica_groups=mesh['feeder'=32,'scen'=16] {'feeder'}, dimensions={0}, use_global_device_ids=true | all-gather | bytes 50688 | tf_op jit(solution)/shard_map/all_gather | solution.py:14
  30.3 1.4 fusion.74
  31.7 24.9 %all-gather.1 = f32[512,24]{1,0:T(8,128)S(1)} all-gather(f32[16,24]{1,0:T(8,128)S(1)} %get-tuple-element.314), channel_id=3, replica_groups=mesh['feeder'=32,'scen'=16] {'feeder'}, dimensions={0}, use_global_device_ids=true | all-gather | bytes 50688 | tf_op jit(solution)/shard_map/all_gather | solution.py:14
  56.7 0.9 fusion.93
  57.6 22.2 %all-gather.2 = f32[512,24]{1,0:T(8,128)S(1)} all-gather(f32[16,24]{1,0:T(8,128)S(1)} %get-tuple-element.320), channel_id=4, replica_groups=mesh['feeder'=32,'scen'=16] {'feeder'}, dimensions={0}, use_global_device_ids=true | all-gather | bytes 50688 | tf_op jit(solution)/shard_map/all_gather | solution.py:14
  80.4 24.7 %all-gather.3 = f32[512,24]{1,0:T(8,128)S(1)} all-gather(f32[16,24]{1,0:T(8,128)S(1)} %get-tuple-element.322), channel_id=5, replica_groups=mesh['feeder'=32,'scen'=16] {'feeder'}, dimensions={0}, use_global_device_ids=true | all-gather | bytes 50688 | tf_op jit(solution)/shard_map/all_gather | solution.py:14
  105.7 22.2 %all-gather.4 = f32[512,24]{1,0:T(8,128)S(1)} all-gather(f32[16,24]{1,0:T(8,128)S(1)} %get-tuple-element.324), channel_id=6, replica_groups=mesh['feeder'=32,'scen'=16] {'feeder'}, dimensions={0}, use_global_device_ids=true | all-gather | bytes 50688 | tf_op jit(solution)/shard_map/all_gather | solution.py:14
  128.5 24.9 %all-gather.5 = f32[512,24]{1,0:T(8,128)S(1)} all-gather(f32[16,24]{1,0:T(8,128)S(1)} %get-tuple-element.326), channel_id=7, replica_groups=mesh['feeder'=32,'scen'=16] {'feeder'}, dimensions={0}, use_global_device_ids=true | all-gather | bytes 50688 | tf_op jit(solution)/shard_map/all_gather | solution.py:14
  153.4 1.4 fusion.97
  154.8 22.2 %all-gather.6 = f32[512,24]{1,0:T(8,128)S(1)} all-gather(f32[16,24]{1,0:T(8,128)S(1)} %get-tuple-element.328), channel_id=8, replica_groups=mesh['feeder'=32,'scen'=16] {'feeder'}, dimensions={0}, use_global_device_ids=true | all-gather | bytes 50688 | tf_op jit(solution)/shard_map/all_gather | solution.py:14
  177.0 1.9 fusion.98
  179.0 24.7 %all-gather.7 = f32[512,24]{1,0:T(8,128)S(1)} all-gather(f32[16,24]{1,0:T(8,128)S(1)} %get-tuple-element.330), channel_id=9, replica_groups=mesh['feeder'=32,'scen'=16] {'feeder'}, dimensions={0}, use_global_device_ids=true | all-gather | bytes 50688 | tf_op jit(solution)/shard_map/all_gather | solution.py:14
  204.3 1.4 broadcast_multiply_fusion
  205.8 0.7 copy-done.6
  206.5 1.0 fusion.48
  208.1 37.2 %all-gather.8 = f32[384,512]{1,0:T(8,128)S(1)} all-gather(f32[24,512]{1,0:T(8,128)S(1)} %bitcast.138), channel_id=10, replica_groups=mesh['feeder'=32,'scen'=16] {'scen'}, dimensions={0}, use_global_device_ids=true | all-gather | bytes 835584 | tf_op jit(solution)/shard_map/all_gather | solution.py:64
  245.7 1.3 dynamic-slice
  248.0 27.5 %all-reduce.3 = (f32[384]{0:T(512)S(1)}, f32[384]{0:T(512)S(1)}, f32[384]{0:T(512)S(1)}) all-reduce(f32[384]{0:T(512)S(1)} %fusion.86, f32[384]{0:T(512)S(1)} %fusion.84, f32[384]{0:T(512)S(1)} %dynamic-update-slice.1), channel_id=11, replica_groups=mesh['feeder'=32,'scen'=16] {'scen'}, use_global_device_ids=true, to_apply=%add | all-reduce | flops 1152 | bytes 9216
  275.7 23.5 %while.30 = (s32[]{:T(128)}, f32[24,512]{1,0:T(8,128)S(1)}, f32[24]{0:T(128)S(1)}, s32[16]{0:T(128)S(1)}, s32[]{:T(128)}, /*index=5*/f32[16,24,512]{2,1,0:T(8,12...) while((s32[]{:T(128)}, f32[24,512]{1,0:T(8,128)S(1)}, ...), condition=%wide.region_18.19_spmd.clone, body=%wide.region_17.18_spmd.clone.sunk | while | flops 49252 | bytes 148175 | solution.py:92
  275.8 0.7 dynamic_slice.91
  280.2 0.7 dynamic_slice.91
  281.6 0.7 dynamic_slice.91
  283.1 0.7 dynamic_slice.91
  287.5 0.7 dynamic_slice.91
  289.0 0.7 dynamic_slice.91
  299.3 32.1 %all_gather.82 = f32[16,24,512]{2,1,0:T(8,128)S(1)} all-gather(f32[1,24,512]{2,1,0:T(8,128)S(1)} %copy.69), channel_id=1, replica_groups=mesh['feeder'=32,'scen'=16] {'scen'}, dimensions={0}, use_global_device_ids=true | all-gather | bytes 835584 | tf_op jit(solution)/shard_map/all_gather | solution.py:66
  331.6 23.5 %while.31 = (s32[]{:T(128)}, f32[24,512]{1,0:T(8,128)S(1)}, f32[24]{0:T(128)S(1)}, s32[16]{0:T(128)S(1)}, s32[]{:T(128)}, /*index=5*/f32[16,24,512]{2,1,0:T(8,12...) while((s32[]{:T(128)}, f32[24,512]{1,0:T(8,128)S(1)}, ...), condition=%wide.region_20.21_spmd.clone, body=%wide.region_19.20_spmd.clone.sunk | while | flops 49253 | bytes 148195 | solution.py:95
  331.6 0.7 dynamic_slice.94
  355.3 0.7 fusion.50
  356.7 1.7 subtract_add_fusion
  (165 shorter events, 27.4 us)
Async XLA Ops:
  0.6 1.4 copy-start.4
  2.0 1.0 copy-start
  3.0 0.7 copy-start.7
  3.4 26.9 %copy-start.2 = (f32[16,24,512]{2,1,0:T(8,128)S(1)}, f32[16,24,512]{2,1,0:T(8,128)}, u32[]{:S(2)}) copy-start(f32[16,24,512]{2,1,0:T(8,128)} %param.15) | copy-start | bytes 2359300
  29.6 0.7 copy-start.5
  203.7 0.7 copy-start.8
  205.7 0.7 copy-start.6
  355.3 1.1 copy-start.1
  355.3 1.4 copy-start.3
